TPU v7x, 128 devices: a whole 4x4x4 slice. The times are simulated.
128 devices in a mesh: gx: 16 (over y, x), yz: 8 (over z, core).
Axes of the slice: x: 4, y: 4, z: 4, core: 2. Of those that a mesh axis runs over, the one named last changes fastest.
Arguments:
- fields: bfloat16 [4, 512, 262144], P(None, 'gx', 'yz'), may hold values from -8 to 8
- test_matrix: float32 [512, 64], replicated, may hold values from -6 to 6
Outputs:
- factor: float32 [512, 64], replicated
- core: bfloat16 [64, 4, 262144], P('gx', None, 'yz')
All inputs are finite; a program needn't handle non-finite values.
Results may differ from a plain program's by a relative error of at most 0.0036.
Values may be sent and summed in bfloat16 or wider, within the bound.
No kernel may reach another device: no remote copies, remote signals or barrier semaphores. Data moves between devices by JAX's collectives and lax.ppermute only.
A program may use at most 192 MiB of HBM per device.

v0:
```python
import jax
import jax.numpy as jnp
from jax import lax
from jax.sharding import PartitionSpec as P


def orthonormal(matrix_y):
    moment = jnp.dot(matrix_y.T, matrix_y, precision=lax.Precision.HIGHEST)
    lower = jnp.linalg.cholesky(moment)
    return lax.linalg.triangular_solve(
        lower, matrix_y, left_side=False, lower=True, transpose_a=True
    )


def body(fields, test_matrix):
    species_count, slab_len, cell_count = fields.shape
    norm_scale = 1.0 / (species_count * cell_count * lax.axis_size("yz"))
    pieces = lax.all_to_all(fields, "gx", split_axis=2, concat_axis=1, tiled=True)
    gram_parts = jnp.einsum("sxc,syc->sxy", pieces, pieces, preferred_element_type=jnp.float32)
    gram_parts, fibres = (gram_parts, pieces)
    local_gram = jnp.sum(gram_parts, axis=0)
    summed_gram = lax.psum(local_gram, ("gx", "yz"))
    sketch = jnp.dot(summed_gram, test_matrix, precision=lax.Precision.HIGHEST) * norm_scale
    factor = orthonormal(orthonormal(sketch))
    factor_low = factor.astype(jnp.bfloat16)
    core_block = jnp.einsum(
        "xr,sxc->rsc", factor_low, fibres, preferred_element_type=jnp.float32
    ).astype(jnp.bfloat16)
    core_block = lax.all_to_all(core_block, "gx", split_axis=0, concat_axis=2, tiled=True)
    return (factor, core_block)


def solution(mesh):
    in_specs = (P(None, "gx", "yz"), P())
    out_specs = (P(), P("gx", None, "yz"))
    return jax.shard_map(body, mesh=mesh, in_specs=in_specs, out_specs=out_specs, check_vma=False)
```

profile of v0, /device:TPU:0, one launch (start us, length us, event | category | flops | bytes accessed | tf_op | source)
XLA Modules:
  0.0 475.0 jit_solution(1052672916725822940)
XLA Ops:
  7.2 0.0 copy-start
  7.2 0.0 all-reduce.2.cloned.1.call-start
  7.2 39.0 %copy.8 = bf16[4,32,32768]{1,0,2:T(4,128)(2,1)} copy(bf16[4,32,32768]{2,1,0:T(8,128)(2,1)} %param.5) | data formatting | bytes 16777216 | tf_op args[0]
  46.2 35.0 %reshape.23 = bf16[16,2,131072]{2,1,0:T(2,128)(2,1)} reshape(bf16[32768,4,32]{2,1,0:T(4,128)(2,1)} %bitcast.50) | data formatting | bytes 16777216
  81.3 103.0 %all_to_all.36 = bf16[16,2,131072]{2,1,0:T(2,128)(2,1)} all-to-all(bf16[16,2,131072]{2,1,0:T(2,128)(2,1)} %reshape.23), channel_id=1, replica_groups=mesh['gx'=16,'yz'=8] {'gx'}, dimensions={0} | all-to-all | bytes 16777216 | tf_op jit(solution)/shard_map/all_to_all | solution.py:18
  184.3 22.9 %reshape.24 = bf16[32768,4,32]{2,1,0:T(4,128)(2,1)} reshape(bf16[16,2,131072]{2,1,0:T(2,128)(2,1)} %all_to_all.36) | data formatting | bytes 16777216
  207.2 45.2 %copy.9 = bf16[4,32,16,2048]{3,1,2,0:T(8,128)(2,1)} copy(bf16[4,32,16,2048]{1,0,3,2:T(4,128)(2,1)} %bitcast.49) | data formatting | bytes 16777216 | tf_op jit(solution)/shard_map/all_to_all | solution.py:18
  252.4 11.3 %convolution_bitcast_fusion = f32[512,512]{1,0:T(8,128)} fusion(bf16[4,512,2048]{2,1,0:T(8,128)(2,1)} %bitcast.51), kind=kOutput, calls=%fused_computation.1 | convolution fusion | flops 4294967296 | bytes 9437184 | tf_op jit(solution)/shard_map/sxc,syc->sxy/dot_general | solution.py:19
  263.7 0.0 all-reduce.2.cloned.1.call-update
  263.7 146.2 %all-reduce.2.cloned.1.call-done = f32[512,512]{1,0:T(8,128)} async-done(((f32[512,512]{1,0:T(8,128)}), f32[512,512]{1,0:T(8,128)}) %all-reduce.2.cloned.1.call-update) | async-done | bytes 1048592 | tf_op jit(solution)/shard_map/psum | solution.py:22
  409.9 0.0 copy-done
  409.9 2.4 convolution_multiply_fusion
  412.3 0.3 fusion.10
  412.5 0.1 copy.10
  412.6 5.8 %cholesky.44 = f32[64,64]{1,0:T(8,128)S(1)} custom-call(f32[64,64]{1,0:T(8,128)S(1)} %fusion.7), custom_call_target="Cholesky" | custom-call | tf_op jit(solution)/shard_map/jit(cholesky)/cholesky | solution.py:9
  418.5 0.6 compare_reduce_fusion.1
  419.1 0.7 fusion.2
  419.8 4.9 %custom-call.6 = f32[1,64,64]{1,2,0:T(8,128)S(1)} custom-call(f32[1,64,64]{2,1,0:T(8,128)S(1)} %fusion.2), custom_call_target="InvertDiagBlocksLowerTriangular" | custom-call | tf_op jit(solution)/shard_map/triangular_solve/custom-call.0 | solution.py:10
  424.7 0.3 convolution_bitcast_fusion.2
  425.0 0.3 fusion.11
  425.3 0.1 copy.11
  425.4 5.8 %cholesky.55 = f32[64,64]{1,0:T(8,128)S(1)} custom-call(f32[64,64]{1,0:T(8,128)S(1)} %fusion.5), custom_call_target="Cholesky" | custom-call | tf_op jit(solution)/shard_map/jit(cholesky)/cholesky | solution.py:9
  431.3 0.6 compare_reduce_fusion
  431.9 0.7 fusion.3
  432.6 4.9 %custom-call.7 = f32[1,64,64]{1,2,0:T(8,128)S(1)} custom-call(f32[1,64,64]{2,1,0:T(8,128)S(1)} %fusion.3), custom_call_target="InvertDiagBlocksLowerTriangular" | custom-call | tf_op jit(solution)/shard_map/triangular_solve/custom-call.0 | solution.py:10
  437.5 0.3 convolution_bitcast_fusion.1
  437.8 0.0 copy-start.1
  437.8 5.0 %convolution_convert_fusion = bf16[64,4,2048]{2,0,1:T(8,128)(2,1)S(1)} fusion(bf16[4,512,2048]{2,1,0:T(8,128)(2,1)} %bitcast.52, f32[512,64]{0,1:T(8,128)S(1)} %convolution_bitcast_fusion.1), kind=kOutput, calls=%fused_computation | convolution fusion | flops 537427968 | bytes 9568256 | tf_op jit(solution)/shard_map/xr,sxc->rsc/dot_general | solution.py:26
  442.9 0.8 copy.12
  443.7 23.0 %all_to_all.37 = bf16[64,4,2048]{2,1,0:T(4,128)(2,1)S(1)} all-to-all(bf16[64,4,2048]{2,1,0:T(4,128)(2,1)S(1)} %copy.12), channel_id=1, replica_groups=mesh['gx'=16,'yz'=8] {'gx'}, dimensions={0} | all-to-all | bytes 2097152 | tf_op jit(solution)/shard_map/all_to_all | solution.py:29
  466.7 1.4 copy.14
  468.1 0.0 copy-done.1
  (4 shorter events, 0.1 us)
Async XLA Ops:
  7.2 402.7 %copy-start = (f32[512,64]{0,1:T(8,128)S(1)}, f32[512,64]{0,1:T(8,128)}, u32[]{:S(2)}) copy-start(f32[512,64]{0,1:T(8,128)} %param.6) | copy-start | bytes 393220
  7.2 402.7 %all-reduce.2.cloned.1.call-start = ((), (), s32[]{:S(2)}) async-start(), calls=%async_computation.2 | async-start | bytes 2097152 | tf_op jit(solution)/shard_map/psum | solution.py:22
  437.8 30.3 %copy-start.1 = (f32[512,64]{0,1:T(8,128)}, f32[512,64]{0,1:T(8,128)S(1)}, u32[]{:S(2)}) copy-start(f32[512,64]{0,1:T(8,128)S(1)} %convolution_bitcast_fusion.1) | copy-start | bytes 393220
Sparse Core Ops, SparseCore 0:
  263.8 145.9 all-reduce.1
where the time goes:
time: 478 us; the launch traced here: 475 us
  waiting for transfers between devices  146 us (31%)
  local copies, waits for them, and re-layouts  145 us (30%)
  blocking collectives  126 us (26%)
  other arithmetic  24.2 us (5%)
  matrix products  19.8 us (4%)
  between operations  14.1 us (3%)
    psum x1, waiting for transfers between devices, body(): summed_gram = lax.psum(local_gram, ('gx', 'yz'))  146 us
    all_to_all x1, blocking collectives, body(): lax.all_to_all(fields, 'gx', split_axis=2, concat_axis=1, tiled=True)  103 us
    unnamed x7, local copies, waits for them, and re-layouts  97 us
    all_to_all x1, local copies, waits for them, and re-layouts, body(): lax.all_to_all(fields, 'gx', split_axis=2, concat_axis=1, tiled=True)  45.2 us
    all_to_all x1, blocking collectives, body(): lax.all_to_all(core_block, 'gx', split_axis=0, concat_axis=2, tiled=True)  23 us
    another operation x6, other arithmetic, orthonormal(): lower = jnp.linalg.cholesky(moment)  13 us
    dot_general x1, matrix products, body(): jnp.einsum('sxc,syc->sxy', pieces, pieces, preferred_element_type=jnp.flo...  11.3 us
    another operation x4, other arithmetic, orthonormal(): lax.linalg.triangular_solve(lower, matrix_y, left_side=False, lower=True,...  11.1 us
  transfers between devices with their start and end apart: 1, of which 1 were waited for; matrix products, arithmetic and copies ran while one was open for 0% of the time, Pallas kernels for 0%

commit v1 on v0

--- a/solution.py
+++ b/solution.py
@@ -2,6 +2,12 @@
 import jax.numpy as jnp
 from jax import lax
 from jax.sharding import PartitionSpec as P
+
+
+def summed_here(x, mesh_axis):
+    shards = lax.all_gather(x, mesh_axis, axis=0, tiled=False)
+    total = shards.sum(axis=0)
+    return total
 
 
 def orthonormal(matrix_y):
@@ -19,7 +25,7 @@
     gram_parts = jnp.einsum("sxc,syc->sxy", pieces, pieces, preferred_element_type=jnp.float32)
     gram_parts, fibres = (gram_parts, pieces)
     local_gram = jnp.sum(gram_parts, axis=0)
-    summed_gram = lax.psum(local_gram, ("gx", "yz"))
+    summed_gram = summed_here(local_gram, ("gx", "yz"))
     sketch = jnp.dot(summed_gram, test_matrix, precision=lax.Precision.HIGHEST) * norm_scale
     factor = orthonormal(orthonormal(sketch))
     factor_low = factor.astype(jnp.bfloat16)

time: 478 us -> 654 us (1.37)
  waiting for transfers between devices: 146 us -> 282 us
  other arithmetic: 24.2 us -> 64.9 us
    all_gather x0 -> x1, waiting for transfers between devices: none -> 282 us  [summed_here(): shards = lax.all_gather(x, mesh_axis, axis=0, tiled=False)]
    psum x1 -> x0, waiting for transfers between devices: 146 us -> none  [body(): summed_gram = lax.psum(local_gram, ('gx', 'yz'))]
    reduce_sum x0 -> x1, other arithmetic: none -> 40.7 us  [summed_here(): total = shards.sum(axis=0)]
where the time goes in v1:
time: 654 us; the launch traced here: 651 us
  waiting for transfers between devices  282 us (43%)
  local copies, waits for them, and re-layouts  145 us (22%)
  blocking collectives  127 us (19%)
  other arithmetic  64.9 us (10%)
  matrix products  18.6 us (3%)
  between operations  14.2 us (2%)
    all_gather x1, waiting for transfers between devices, summed_here(): shards = lax.all_gather(x, mesh_axis, axis=0, tiled=False)  282 us
    all_to_all x1, blocking collectives, body(): lax.all_to_all(fields, 'gx', split_axis=2, concat_axis=1, tiled=True)  103 us
    unnamed x7, local copies, waits for them, and re-layouts  97 us
    all_to_all x1, local copies, waits for them, and re-layouts, body(): lax.all_to_all(fields, 'gx', split_axis=2, concat_axis=1, tiled=True)  45.3 us
    reduce_sum x1, other arithmetic, summed_here(): total = shards.sum(axis=0)  40.7 us
    all_to_all x1, blocking collectives, body(): lax.all_to_all(core_block, 'gx', split_axis=0, concat_axis=2, tiled=True)  24.2 us
  transfers between devices with their start and end apart: 1, of which 1 were waited for; matrix products, arithmetic and copies ran while one was open for 0% of the time, Pallas kernels for 0%

profile of v1, /device:TPU:0, one launch (start us, length us, event | category | flops | bytes accessed | tf_op | source)
XLA Modules:
  0.0 651.4 jit_solution(11102270385642201909)
XLA Ops:
  7.2 0.0 copy-start
  7.2 0.0 all-gather.3.cloned.1.call-start
  7.2 39.0 %copy.8 = bf16[4,32,32768]{1,0,2:T(4,128)(2,1)} copy(bf16[4,32,32768]{2,1,0:T(8,128)(2,1)} %param.5) | data formatting | bytes 16777216 | tf_op args[0]
  46.2 35.0 %reshape.24 = bf16[16,2,131072]{2,1,0:T(2,128)(2,1)} reshape(bf16[32768,4,32]{2,1,0:T(4,128)(2,1)} %bitcast.51) | data formatting | bytes 16777216
  81.3 103.0 %all_to_all.36 = bf16[16,2,131072]{2,1,0:T(2,128)(2,1)} all-to-all(bf16[16,2,131072]{2,1,0:T(2,128)(2,1)} %reshape.24), channel_id=1, replica_groups=mesh['gx'=16,'yz'=8] {'gx'}, dimensions={0} | all-to-all | bytes 16777216 | tf_op jit(solution)/shard_map/all_to_all | solution.py:24
  184.3 22.9 %reshape.25 = bf16[32768,4,32]{2,1,0:T(4,128)(2,1)} reshape(bf16[16,2,131072]{2,1,0:T(2,128)(2,1)} %all_to_all.36) | data formatting | bytes 16777216
  207.2 45.3 %copy.9 = bf16[4,32,16,2048]{3,1,2,0:T(8,128)(2,1)} copy(bf16[4,32,16,2048]{1,0,3,2:T(4,128)(2,1)} %bitcast.50) | data formatting | bytes 16777216 | tf_op jit(solution)/shard_map/all_to_all | solution.py:24
  252.5 11.3 %convolution_bitcast_fusion = f32[512,512]{1,0:T(8,128)} fusion(bf16[4,512,2048]{2,1,0:T(8,128)(2,1)} %bitcast.52), kind=kOutput, calls=%fused_computation.1 | convolution fusion | flops 4294967296 | bytes 9437184 | tf_op jit(solution)/shard_map/sxc,syc->sxy/dot_general | solution.py:25
  263.7 0.0 all-gather.3.cloned.1.call-update
  263.8 281.9 %all-gather.3.cloned.1.call-done = f32[65536,512]{1,0:T(8,128)} async-done(((f32[512,512]{1,0:T(8,128)}), f32[65536,512]{1,0:T(8,128)}) %all-gather.3.cloned.1.call-update) | async-done | bytes 134217744 | tf_op jit(solution)/shard_map/all_gather | solution.py:8
  545.7 40.7 %reduce_sum.8 = f32[512,512]{1,0:T(8,128)S(1)} reduce(f32[128,512,512]{2,1,0:T(8,128)} %bitcast.4, f32[]{:T(128)} %constant.31.clone.1), dimensions={0}, to_apply=%region_0.0 | reduce | flops 33292288 | bytes 135266304 | tf_op jit(solution)/shard_map/reduce_sum | solution.py:9
  586.4 0.0 copy-done
  586.4 1.1 convolution_multiply_fusion
  587.5 0.3 fusion.10
  587.8 0.1 copy.10
  587.9 5.8 cholesky.44
  593.8 0.6 compare_reduce_fusion.1
  594.4 0.7 fusion.2
  595.1 4.9 custom-call.6
  600.0 0.3 convolution_bitcast_fusion.2
  600.3 0.3 fusion.11
  600.6 0.1 copy.11
  600.7 5.8 cholesky.55
  606.6 0.6 compare_reduce_fusion
  607.2 0.7 fusion.3
  607.9 4.9 custom-call.7
  612.8 0.3 convolution_bitcast_fusion.1
  613.1 0.0 copy-start.1
  613.1 5.0 convolution_convert_fusion
  618.1 0.8 copy.12
  619.0 24.2 %all_to_all.37 = bf16[64,4,2048]{2,1,0:T(4,128)(2,1)S(1)} all-to-all(bf16[64,4,2048]{2,1,0:T(4,128)(2,1)S(1)} %copy.12), channel_id=1, replica_groups=mesh['gx'=16,'yz'=8] {'gx'}, dimensions={0} | all-to-all | bytes 2097152 | tf_op jit(solution)/shard_map/all_to_all | solution.py:35
  643.1 1.4 copy.14
  644.6 0.0 copy-done.1
  (4 shorter events, 0.1 us)
Async XLA Ops:
  7.2 579.2 %copy-start = (f32[512,64]{0,1:T(8,128)S(1)}, f32[512,64]{0,1:T(8,128)}, u32[]{:S(2)}) copy-start(f32[512,64]{0,1:T(8,128)} %param.6) | copy-start | bytes 393220
  7.2 538.5 %all-gather.3.cloned.1.call-start = ((), (), s32[]{:S(2)}) async-start(), calls=%async_computation.2 | async-start | bytes 135266304 | tf_op jit(solution)/shard_map/all_gather | solution.py:8
  613.1 31.5 %copy-start.1 = (f32[512,64]{0,1:T(8,128)}, f32[512,64]{0,1:T(8,128)S(1)}, u32[]{:S(2)}) copy-start(f32[512,64]{0,1:T(8,128)S(1)} %convolution_bitcast_fusion.1) | copy-start | bytes 393220
Sparse Core Ops, SparseCore 0:
  263.9 281.7 all-gather.2
